TPU v7x, 768 devices: a whole 4x8x12 slice. The times are simulated.
768 devices in a mesh: seq: 16 (over y, core), head: 48 (over x, z).
Axes of the slice: x: 4, y: 8, z: 12, core: 2. Of those that a mesh axis runs over, the one named last changes fastest.
Arguments:
- query_rows: bfloat16 [6144, 6144], P('seq', 'head'), may hold values from -6 to 6
- key_rows: bfloat16 [8192, 6144], P('seq', 'head'), may hold values from -6 to 6
- value_rows: bfloat16 [8192, 6144], P('seq', 'head'), may hold values from -6 to 6
- attn_out: bfloat16 [6144, 6144], P(('seq', 'head')), may hold values from -3 to 3
- out_grad: bfloat16 [6144, 6144], P(('seq', 'head')), may hold values from -48 to 48
- logsumexp: bfloat16 [48, 6144], P('head', 'seq'), may hold values from 4.5 to 6.5
- shard_pick: int32 [48, 6144, 4], P('head', 'seq'), may hold values from 0 to 15, all different within a row; in each aligned block of 384 rows (0 to 383, 384 to 767, ..., all dimensions but the last counted through in order) at most 192 rows name the same one
- block_pick: int32 [48, 6144, 4, 4], P('head', 'seq'), may hold values from 0 to 7, as said below
Outputs:
- query_grad: bfloat16 [6144, 6144], P('seq', 'head')
- key_grad: bfloat16 [8192, 6144], P('seq', 'head')
- value_grad: bfloat16 [8192, 6144], P('seq', 'head')
Inputs may be any that keep to these rules, and one draw needn't show every extreme that they name: `shard_pick`: each query row of each head names 4 different shards; among the 384 rows of one device (one head, one shard of query rows) no shard is named more than 192 times. `block_pick`: the 4 entries of one query row, head and group are different.
All inputs are finite; a program needn't handle non-finite values.
Results may differ from a plain program's by a relative error of at most 0.0077.
Values may be sent and summed in bfloat16 or wider, within the bound.
A program may use at most 32 MiB of HBM per device.

v0:
```python
import jax
import jax.numpy as jnp
from jax import lax
from jax.sharding import PartitionSpec as P

BLK = 64


def block_terms(row_data, small_data, key_rows, value_rows, own_shard, groups):
    count = row_data.shape[0]
    head_size = key_rows.shape[1]
    per_shard = key_rows.shape[0] // BLK
    queries = row_data[:, :head_size]
    grads = row_data[:, head_size:]
    stats = small_data[:, :2].astype(jnp.float32)
    shards_of = small_data[:, 2 : 2 + groups].astype(jnp.int32)
    picks_of = small_data[:, 2 + groups :].astype(jnp.int32).reshape(count, groups, -1)
    local_ids = jnp.arange(per_shard, dtype=jnp.int32)
    matched = (shards_of == own_shard + 1)[:, :, None, None] & (
        picks_of[:, :, :, None] == local_ids[None, None, None, :]
    )
    chosen = jnp.any(matched, axis=(1, 2))
    mask = jnp.broadcast_to(chosen[:, :, None], (count, per_shard, BLK)).reshape(
        count, key_rows.shape[0]
    )
    scores = jnp.dot(queries, key_rows.T, preferred_element_type=jnp.float32) * head_size ** (-0.5)
    probs = jnp.where(mask, jnp.exp(scores - stats[:, 0:1]), 0.0)
    probs_low = probs.astype(jnp.bfloat16)
    value_add = jnp.dot(probs_low.T, grads, preferred_element_type=jnp.float32)
    dprob = jnp.dot(grads, value_rows.T, preferred_element_type=jnp.float32)
    dscore = (probs * (dprob - stats[:, 1:2])).astype(jnp.bfloat16)
    key_add = jnp.dot(dscore.T, queries, preferred_element_type=jnp.float32)
    query_part = jnp.dot(dscore, key_rows, preferred_element_type=jnp.float32)
    return (query_part, key_add, value_add)


def sweep(rows_in, small_in, key_rows, value_rows, own_shard, groups):
    sources, per_source = (rows_in.shape[0], rows_in.shape[1])
    merged = 1
    while merged * 2 <= sources and sources % (merged * 2) == 0 and (merged * per_source < 512):
        merged = merged * 2
    rows_blocks = rows_in.reshape(sources // merged, merged * per_source, rows_in.shape[2])
    small_blocks = small_in.reshape(sources // merged, merged * per_source, small_in.shape[2])
    zeros_kv = jnp.zeros(key_rows.shape, jnp.float32)

    def advance(carry, pieces):
        query_part, key_add, value_add = block_terms(
            pieces[0], pieces[1], key_rows, value_rows, own_shard, groups
        )
        return ((carry[0] + key_add, carry[1] + value_add), query_part)

    (key_sum, value_sum), query_parts = lax.scan(
        advance, (zeros_kv, zeros_kv), (rows_blocks, small_blocks)
    )
    return (query_parts.reshape(sources, per_source, -1), key_sum, value_sum)


def local(query_rows, key_rows, value_rows, attn_out, out_grad, logsumexp, shard_pick, block_pick):
    head_size = query_rows.shape[1]
    q_count = query_rows.shape[0]
    scale = head_size ** (-0.5)
    out_local, grad_local = (
        lax.all_to_all(attn_out, "head", split_axis=1, concat_axis=0, tiled=True),
        lax.all_to_all(out_grad, "head", split_axis=1, concat_axis=0, tiled=True),
    )
    delta = jnp.sum(
        out_local.astype(jnp.float32) * grad_local.astype(jnp.float32), axis=1, keepdims=True
    ).astype(jnp.bfloat16)
    seq_count = lax.axis_size("seq")
    own_shard = lax.axis_index("seq")
    targets = shard_pick[0]
    groups = targets.shape[1]
    picks = block_pick[0].reshape(q_count, -1)
    row_data = jnp.concatenate([query_rows, grad_local], axis=1)
    small_data = jnp.concatenate(
        [
            logsumexp[0][:, None],
            delta,
            (targets + 1).astype(jnp.bfloat16),
            picks.astype(jnp.bfloat16),
        ],
        axis=1,
    )
    capacity = min(q_count, 2 * q_count * groups // seq_count)
    shard_ids = jnp.arange(seq_count, dtype=jnp.int32)
    hits = jnp.any(targets[:, :, None] == shard_ids[None, None, :], axis=1).astype(jnp.float32)
    row_ids = jnp.arange(q_count, dtype=jnp.int32)
    lower = (row_ids[:, None] >= row_ids[None, :]).astype(jnp.float32)
    slots = (
        jnp.dot(lower, hits, precision=lax.Precision.HIGHEST, preferred_element_type=jnp.float32)
        - 1.0
    )
    slot_ids = jnp.arange(capacity, dtype=jnp.float32)
    dispatch = hits.T[:, None, :] * (slots.T[:, None, :] == slot_ids[None, :, None]).astype(
        jnp.float32
    )
    dispatch_low = dispatch.astype(jnp.bfloat16)
    send_rows = jnp.einsum(
        "scr,rf->scf", dispatch_low, row_data, preferred_element_type=jnp.float32
    ).astype(jnp.bfloat16)
    send_small = jnp.einsum(
        "scr,rf->scf", dispatch_low, small_data, preferred_element_type=jnp.float32
    ).astype(jnp.bfloat16)
    got_rows, got_small = (
        lax.all_to_all(send_rows, "seq", split_axis=0, concat_axis=0, tiled=True),
        lax.all_to_all(send_small, "seq", split_axis=0, concat_axis=0, tiled=True),
    )
    query_parts, key_sum, value_sum = sweep(
        got_rows, got_small, key_rows, value_rows, own_shard, groups
    )
    returned = lax.all_to_all(query_parts, "seq", split_axis=0, concat_axis=0, tiled=True)
    total = jnp.einsum(
        "scr,scd->rd",
        dispatch,
        returned,
        precision=lax.Precision.HIGHEST,
        preferred_element_type=jnp.float32,
    )
    query_grad = (total * scale).astype(jnp.bfloat16)
    key_grad = (key_sum * scale).astype(jnp.bfloat16)
    value_grad = value_sum.astype(jnp.bfloat16)
    return (query_grad, key_grad, value_grad)


def solution(mesh):
    placed = (
        P("seq", "head"),
        P("seq", "head"),
        P("seq", "head"),
        P(("seq", "head"), None),
        P(("seq", "head"), None),
        P("head", "seq"),
        P("head", "seq", None),
        P("head", "seq", None, None),
    )
    return jax.shard_map(
        local,
        mesh=mesh,
        in_specs=placed,
        out_specs=(P("seq", "head"), P("seq", "head"), P("seq", "head")),
        check_vma=False,
    )
```

profile of v0, /device:TPU:1, one launch (start us, length us, event | category | flops | bytes accessed | tf_op | source)
XLA Modules:
  0.0 179.0 jit_solution(14391845277327640845)
XLA Ops:
  0.6 18.9 %all-to-all-start = ((bf16[8,48,128]{2,0,1:T(8,128)(2,1)}), bf16[8,48,128]{2,0,1:T(8,128)(2,1)S(1)}, u32[]{:S(2)}, u32[]{:S(2)}) async-start(bf16[8,48,128]{2,0,1:T(8,128)(2,1)} %bitcast.73), calls=%async_computation | async-start | bytes 196608 | tf_op jit(solution)/shard_map/all_to_all | solution.py:63
  19.5 0.7 fusion.35
  20.2 11.1 %all-to-all-done = bf16[8,48,128]{2,0,1:T(8,128)(2,1)S(1)} async-done(((bf16[8,48,128]{2,0,1:T(8,128)(2,1)}), bf16[8,48,128]{2,0,1:T(8,128)(2,1)S(1)}, u32[]{:S(2)}, u32[]{:S(2)}) %all-to-all-start) | async-done | bytes 98336 | tf_op jit(solution)/shard_map/all_to_all | solution.py:63
  31.4 4.5 %all-to-all-start.1 = ((bf16[8,48,128]{2,0,1:T(8,128)(2,1)}), bf16[8,48,128]{2,0,1:T(8,128)(2,1)S(1)}, u32[]{:S(2)}, u32[]{:S(2)}) async-start(bf16[8,48,128]{2,0,1:T(8,128)(2,1)} %bitcast.74), calls=%async_computation.1 | async-start | bytes 196608 | tf_op jit(solution)/shard_map/all_to_all | solution.py:64
  35.9 0.7 add_convert_fusion
  36.6 0.7 convert_element_type.93
  37.5 10.3 %all-to-all-done.1 = bf16[8,48,128]{2,0,1:T(8,128)(2,1)S(1)} async-done(((bf16[8,48,128]{2,0,1:T(8,128)(2,1)}), bf16[8,48,128]{2,0,1:T(8,128)(2,1)S(1)}, u32[]{:S(2)}, u32[]{:S(2)}) %all-to-all-start.1) | async-done | bytes 98336 | tf_op jit(solution)/shard_map/all_to_all | solution.py:64
  48.0 2.3 %fusion.22 = bf16[16,192,22]{1,2,0:T(8,128)(2,1)} fusion(f32[16,384]{1,0:T(8,128)S(1)} %convert_bitcast_fusion, f32[16,384]{1,0:T(8,128)S(1)} %convolution_add_fusion.2, bf16[384,16]{0,1:T(8,128)(2,1)S(1)} %convert_element_type.94, bf16[384,4]{0,1:T(4,128)(2,1)S(1)} %add_convert_fusion, bf16[384,1]{0,1:T(2,128)(2,1)S(1)} %convert_element_type.91, ...), kind=kOutput, calls=%fused_computation.37 | convolution fusion | flops 54398976 | bytes 201216 | tf_op jit(solution)/shard_map/scr,rf->scf/dot_general | solution.py:101
  50.3 10.7 %all-to-all-start.2 = ((bf16[16,192,22]{1,2,0:T(8,128)(2,1)}), bf16[16,192,22]{1,2,0:T(8,128)(2,1)S(1)}, u32[]{:S(2)}, u32[]{:S(2)}) async-start(bf16[16,192,22]{1,2,0:T(8,128)(2,1)} %fusion.22), calls=%async_computation.2 | async-start | bytes 393216 | tf_op jit(solution)/shard_map/all_to_all | solution.py:106
  61.0 2.1 %fusion.21 = bf16[16,192,256]{2,1,0:T(8,128)(2,1)} fusion(f32[16,384]{1,0:T(8,128)S(1)} %convert_bitcast_fusion, f32[16,384]{1,0:T(8,128)S(1)} %convolution_add_fusion.2, bf16[384,128]{1,0:T(8,128)(2,1)S(1)} %bitcast.72, bf16[384,128]{1,0:T(8,128)(2,1)S(1)} %copy-done.2), kind=kOutput, calls=%fused_computation.36 | convolution fusion | flops 607518720 | bytes 1818624 | tf_op jit(solution)/shard_map/scr,rf->scf/dot_general | solution.py:98
  63.1 8.2 %all-to-all-done.2 = bf16[16,192,22]{1,2,0:T(8,128)(2,1)S(1)} async-done(((bf16[16,192,22]{1,2,0:T(8,128)(2,1)}), bf16[16,192,22]{1,2,0:T(8,128)(2,1)S(1)}, u32[]{:S(2)}, u32[]{:S(2)}) %all-to-all-start.2) | async-done | bytes 135200 | tf_op jit(solution)/shard_map/all_to_all | solution.py:106
  71.3 3.6 %all-to-all-start.3 = ((bf16[16,192,256]{2,1,0:T(8,128)(2,1)}), bf16[16,192,256]{2,1,0:T(8,128)(2,1)S(1)}, u32[]{:S(2)}, u32[]{:S(2)}) async-start(bf16[16,192,256]{2,1,0:T(8,128)(2,1)} %fusion.21), calls=%async_computation.3 | async-start | bytes 3145728 | tf_op jit(solution)/shard_map/all_to_all | solution.py:105
  75.3 37.7 %all-to-all-done.3 = bf16[16,192,256]{2,1,0:T(8,128)(2,1)S(1)} async-done(((bf16[16,192,256]{2,1,0:T(8,128)(2,1)}), bf16[16,192,256]{2,1,0:T(8,128)(2,1)S(1)}, u32[]{:S(2)}, u32[]{:S(2)}) %all-to-all-start.3) | async-done | bytes 1572896 | tf_op jit(solution)/shard_map/all_to_all | solution.py:105
  113.0 15.1 %while.17 = (s32[]{:T(128)}, f32[512,128]{1,0:T(8,128)S(1)}, f32[512,128]{1,0:T(8,128)S(1)}, f32[4,768,128]{2,1,0:T(8,128)}, bf16[4,768,22]{1,2,0:T(8,128)(2,1)S...) while((s32[]{:T(128)}, f32[512,128]{1,0:T(8,128)S(1)}, ...), condition=%wide.region_4.5_spmd.clone, body=%wide.region_2.4_spmd.clone.sunk | while | flops 506639872 | bytes 12401808 | solution.py:52
  113.3 0.5 copy.24
  113.8 0.5 exponential_select_fusion.2
  115.6 1.1 fusion.77
  117.0 0.5 copy.24
  117.6 0.5 exponential_select_fusion.2
  119.4 1.1 fusion.77
  120.8 0.5 copy.24
  121.3 0.5 exponential_select_fusion.2
  121.9 0.4 convolution_add_fusion.6
  123.2 1.1 fusion.77
  124.6 0.5 copy.24
  125.1 0.5 exponential_select_fusion.2
  126.9 1.1 fusion.77
  128.1 4.3 %all-to-all-start.4 = ((f32[16,192,128]{2,1,0:T(8,128)}), f32[16,192,128]{2,1,0:T(8,128)S(1)}, u32[]{:S(2)}, u32[]{:S(2)}) async-start(f32[16,192,128]{2,1,0:T(8,128)} %bitcast.71), calls=%async_computation.4 | async-start | bytes 3145728 | tf_op jit(solution)/shard_map/all_to_all | solution.py:111
  132.4 0.7 convert_element_type.99
  133.1 0.7 multiply_convert_fusion.1
  133.7 37.1 %all-to-all-done.4 = f32[16,192,128]{2,1,0:T(8,128)S(1)} async-done(((f32[16,192,128]{2,1,0:T(8,128)}), f32[16,192,128]{2,1,0:T(8,128)S(1)}, u32[]{:S(2)}, u32[]{:S(2)}) %all-to-all-start.4) | async-done | bytes 1572896 | tf_op jit(solution)/shard_map/all_to_all | solution.py:111
  170.8 8.1 %fusion.29 = bf16[384,128]{1,0:T(8,128)(2,1)} fusion(f32[16,192,128]{2,1,0:T(8,128)S(1)} %all-to-all-done.4, f32[16,384]{1,0:T(8,128)S(1)} %convert_bitcast_fusion, f32[16,384]{1,0:T(8,128)S(1)} %convolution_add_fusion.2), kind=kOutput, calls=%fused_computation.40 | convolution fusion | flops 1814396928 | bytes 1720320 | tf_op jit(solution)/shard_map/scr,scd->rd/dot_general | solution.py:112
  (64 shorter events, 6.4 us)
Async XLA Ops:
  0.6 30.7 %all-to-all-start = ((bf16[8,48,128]{2,0,1:T(8,128)(2,1)}), bf16[8,48,128]{2,0,1:T(8,128)(2,1)S(1)}, u32[]{:S(2)}, u32[]{:S(2)}) async-start(bf16[8,48,128]{2,0,1:T(8,128)(2,1)} %bitcast.73), calls=%async_computation | async-start | bytes 196608 | tf_op jit(solution)/shard_map/all_to_all | solution.py:63
  31.4 16.4 %all-to-all-start.1 = ((bf16[8,48,128]{2,0,1:T(8,128)(2,1)}), bf16[8,48,128]{2,0,1:T(8,128)(2,1)S(1)}, u32[]{:S(2)}, u32[]{:S(2)}) async-start(bf16[8,48,128]{2,0,1:T(8,128)(2,1)} %bitcast.74), calls=%async_computation.1 | async-start | bytes 196608 | tf_op jit(solution)/shard_map/all_to_all | solution.py:64
  48.0 13.0 %copy-start.2 = (bf16[384,128]{1,0:T(8,128)(2,1)S(1)}, bf16[384,128]{1,0:T(8,128)(2,1)}, u32[]{:S(2)}) copy-start(bf16[384,128]{1,0:T(8,128)(2,1)} %param.10) | copy-start | bytes 294916
  50.3 21.0 %all-to-all-start.2 = ((bf16[16,192,22]{1,2,0:T(8,128)(2,1)}), bf16[16,192,22]{1,2,0:T(8,128)(2,1)S(1)}, u32[]{:S(2)}, u32[]{:S(2)}) async-start(bf16[16,192,22]{1,2,0:T(8,128)(2,1)} %fusion.22), calls=%async_computation.2 | async-start | bytes 393216 | tf_op jit(solution)/shard_map/all_to_all | solution.py:106
  63.1 49.8 %copy-start = (bf16[512,128]{1,0:T(8,128)(2,1)S(1)}, bf16[512,128]{1,0:T(8,128)(2,1)}, u32[]{:S(2)}) copy-start(bf16[512,128]{1,0:T(8,128)(2,1)} %param.11) | copy-start | bytes 393220
  63.1 49.8 %copy-start.1 = (bf16[512,128]{1,0:T(8,128)(2,1)S(1)}, bf16[512,128]{1,0:T(8,128)(2,1)}, u32[]{:S(2)}) copy-start(bf16[512,128]{1,0:T(8,128)(2,1)} %param.12) | copy-start | bytes 393220
  71.3 41.6 %all-to-all-start.3 = ((bf16[16,192,256]{2,1,0:T(8,128)(2,1)}), bf16[16,192,256]{2,1,0:T(8,128)(2,1)S(1)}, u32[]{:S(2)}, u32[]{:S(2)}) async-start(bf16[16,192,256]{2,1,0:T(8,128)(2,1)} %fusion.21), calls=%async_computation.3 | async-start | bytes 3145728 | tf_op jit(solution)/shard_map/all_to_all | solution.py:105
  128.1 42.8 %all-to-all-start.4 = ((f32[16,192,128]{2,1,0:T(8,128)}), f32[16,192,128]{2,1,0:T(8,128)S(1)}, u32[]{:S(2)}, u32[]{:S(2)}) async-start(f32[16,192,128]{2,1,0:T(8,128)} %bitcast.71), calls=%async_computation.4 | async-start | bytes 3145728 | tf_op jit(solution)/shard_map/all_to_all | solution.py:111
where the time goes:
time: 180 us; the launch traced here: 179 us
  waiting for transfers between devices  104 us (58%)
  starting transfers between devices  42 us (23%)
  matrix products  24.3 us (14%)
  other arithmetic  4.08 us (2%)
  local copies, waits for them, and re-layouts  3.06 us (2%)
    all_to_all x1, waiting for transfers between devices, local(): lax.all_to_all(send_rows, 'seq', split_axis=0, concat_axis=0, tiled=True)  37.7 us
    all_to_all x1, waiting for transfers between devices, local(): lax.all_to_all(query_parts, 'seq', split_axis=0, concat_axis=0, tiled=True)  37.1 us
    all_to_all x1, starting transfers between devices, local(): lax.all_to_all(attn_out, 'head', split_axis=1, concat_axis=0, tiled=True)  18.9 us
    all_to_all x1, waiting for transfers between devices, local(): lax.all_to_all(attn_out, 'head', split_axis=1, concat_axis=0, tiled=True)  11.1 us
    all_to_all x1, starting transfers between devices, local(): lax.all_to_all(send_small, 'seq', split_axis=0, concat_axis=0, tiled=True)  10.7 us
    all_to_all x1, waiting for transfers between devices, local(): lax.all_to_all(out_grad, 'head', split_axis=1, concat_axis=0, tiled=True)  10.3 us
    all_to_all x1, waiting for transfers between devices, local(): lax.all_to_all(send_small, 'seq', split_axis=0, concat_axis=0, tiled=True)  8.19 us
    dot_general x1, matrix products, local(): jnp.einsum('scr,scd->rd', dispatch, returned, precision=lax.Precision.HIG...  8.13 us
  transfers between devices with their start and end apart: 5, of which 5 were waited for; matrix products, arithmetic and copies ran while one was open for 3% of the time, Pallas kernels for 0%

commit v1 on v0

v1 whole, which is shorter than its diff:
```python
import functools
import math

import jax
import jax.numpy as jnp
from jax import lax
from jax.experimental import pallas as pl
from jax.experimental.pallas import tpu as pltpu
from jax.sharding import PartitionSpec as P

BLK = 64
RING = 8
LOG2E = math.log2(math.e)
NT = (((1,), (1,)), ((), ()))


def kernel(
    n_head, q_hbm, k_hbm, v_hbm, o_hbm, g_hbm, lse_hbm, sp_hbm, bp_hbm,
    dq_hbm, dk_hbm, dv_hbm,
    qb, gb, kx, vx, kt, o_v, g_v, lse_v, sp_v, bp_v, msg, rcv,
    pt, part, pr, sl, rl, dk_acc, dv_acc, dq_v, dk_v, dv_v,
    in_sem, a2a_send, a2a_recv,
    q_send, q_recv, q_ssend, q_srecv,
    g_send, g_recv, g_ssend, g_srecv,
    p_send, p_recv, c_send, c_recv, out_sem,
):
    rows, dh = q_hbm.shape
    q_rows, g_rows = qb.shape[2], gb.shape[2]
    tiles = rows // 128
    per_shard = kx.shape[0] // BLK
    r = rows // n_head
    half = dh // 2
    own = lax.axis_index("seq")
    head = lax.axis_index("head")
    chip, core = own // 2, own % 2
    right = {"seq": ((chip + 1) % RING) * 2 + core}
    left = {"seq": ((chip + RING - 1) % RING) * 2 + core}
    sib = {"seq": chip * 2 + (1 - core)}
    dirs = (right, left)
    scale = dh ** (-0.5)

    loads = [
        pltpu.make_async_copy(src, dst, in_sem.at[i])
        for i, (src, dst) in enumerate(
            (
                (q_hbm, qb.at[0, 0, pl.ds(0, rows)]),
                (o_hbm, o_v),
                (g_hbm, g_v),
                (lse_hbm, lse_v),
                (sp_hbm, sp_v),
                (bp_hbm, bp_v),
                (k_hbm, kx),
                (v_hbm, vx),
            )
        )
    ]
    for load in loads:
        load.start()

    barrier = pltpu.get_barrier_semaphore()
    for peer in (right, left, sib):
        pl.semaphore_signal(barrier, inc=1, device_id=peer)

    def greet(j, _):
        pl.semaphore_signal(barrier, inc=1, device_id={"head": (head + j) % n_head})
        return 0

    lax.fori_loop(1, n_head, greet, 0)

    for load in loads[:6]:
        load.wait()

    lse = lse_v[...].astype(jnp.float32)
    for t in range(tiles):
        cols = pl.ds(t * 128, 128)
        ids = [sp_v[g : g + 1, cols] * per_shard + bp_v[g, :, cols] for g in range(sp_v.shape[0])]
        ids = jnp.concatenate(ids, axis=0).astype(jnp.float32).astype(jnp.bfloat16)
        qb[0, 0, pl.ds(rows + 16 * t, 16), :] = ids
    sub = lax.broadcasted_iota(jnp.int32, (16, 128), 0)

    def lane_tiles(vec):
        out = jnp.broadcast_to(vec[:, 0:128], (16, 128))
        for t in range(1, tiles):
            out = jnp.where(sub == t, jnp.broadcast_to(vec[:, t * 128 : (t + 1) * 128], (16, 128)), out)
        return out.astype(jnp.bfloat16)

    qb[0, 0, pl.ds(rows + 16 * tiles, 16), :] = lane_tiles(lse)
    for h in range(n_head):
        cols = pl.ds(h * dh, dh)
        msg[h, pl.ds(0, r), :] = g_v[:, cols]
        msg[h, pl.ds(r, r), :] = o_v[:, cols]

    def span(buf, h):
        size = buf.shape[2] // 2 // 16 * 16
        return pl.ds(0, size) if h == 0 else pl.ds(size, buf.shape[2] - size)

    def slot(side, d):
        return d if side == 0 else (RING - d) % RING

    def ring(buf, send, recv, side, d, h):
        return pltpu.make_async_remote_copy(
            src_ref=buf.at[0, slot(side, d), span(buf, h)],
            dst_ref=buf.at[0, slot(side, d + 1), span(buf, h)],
            send_sem=send.at[side, d, h],
            recv_sem=recv.at[side, d + 1, h],
            device_id=dirs[side],
        )

    def ring_arrived(buf, send, recv, side, d, h):
        ring(buf, send, recv, side, d - 1, h).wait_recv()

    def twin(buf, send, recv, k):
        return pltpu.make_async_remote_copy(
            src_ref=buf.at[0, k],
            dst_ref=buf.at[1, k],
            send_sem=send.at[k],
            recv_sem=recv.at[k],
            device_id=sib,
        )

    def start_own(buf, send, recv, ssend, srecv):
        for h in range(2):
            for side in range(2):
                ring(buf, send, recv, side, 0, h).start()
        twin(buf, ssend, srecv, 0).start()

    def relay(buf, send, recv, ssend, srecv, d):
        @pl.when((d >= 1) & (d < 4))
        def _():
            for h in range(2):
                for side in range(2):
                    ring_arrived(buf, send, recv, side, d, h)
                    if h == side:
                        ring(buf, send, recv, side, d, h).start()
                    else:
                        @pl.when(d < 3)
                        def _():
                            ring(buf, send, recv, side, d, h).start()
            for side in range(2):
                twin(buf, ssend, srecv, slot(side, d)).start()

        @pl.when(d == 4)
        def _():
            for side in range(2):
                ring_arrived(buf, send, recv, side, 4, side)
            twin(buf, ssend, srecv, 4).start()

    def drain(buf, send, recv, ssend, srecv):
        def per_distance(d, _):
            for side in range(2):
                for h in range(2):
                    if h == side:
                        ring(buf, send, recv, side, d, h).wait_send()
                    else:
                        @pl.when(d < 3)
                        def _():
                            ring(buf, send, recv, side, d, h).wait_send()
            return 0

        lax.fori_loop(0, 4, per_distance, 0)

        def per_slot(k, _):
            twin(buf, ssend, srecv, k).wait_send()
            return 0

        lax.fori_loop(0, RING, per_slot, 0)

    def visit(d, ssend, srecv, buf, compute):
        def one(j, _):
            par, side = j // 2, j % 2
            k = jnp.where(side == 0, d, (RING - d) % RING)

            @pl.when((side == 0) | ((d >= 1) & (d < 4)))
            def _():
                @pl.when(par == 1)
                def _():
                    twin(buf, ssend, srecv, k).wait_recv()

                compute(par, k)

            return 0

        lax.fori_loop(0, 4, one, 0)

    pl.semaphore_wait(barrier, n_head - 1 + 3)
    q_ring = (qb, q_send, q_recv, q_ssend, q_srecv)
    g_ring = (gb, g_send, g_recv, g_ssend, g_srecv)

    def a2a(j, _):
        peer = (head + j) % n_head
        pltpu.make_async_remote_copy(
            src_ref=msg.at[peer],
            dst_ref=rcv.at[head],
            send_sem=a2a_send,
            recv_sem=a2a_recv,
            device_id={"head": peer},
        ).start()
        return 0

    start_own(*q_ring)
    lax.fori_loop(1, n_head, a2a, 0)
    pltpu.make_async_copy(msg.at[head], rcv.at[head], a2a_recv).start()

    for load in loads[6:]:
        load.wait()
    kt[...] = kx[...].astype(jnp.float32).T.astype(jnp.bfloat16)
    dk_acc[...] = jnp.zeros_like(dk_acc)
    dv_acc[...] = jnp.zeros_like(dv_acc)

    def row_of_tiles(tile):
        return jnp.concatenate([tile[t : t + 1, :] for t in range(tiles)], axis=1)

    def probs(par, k):
        s = lax.dot_general(kx[...], qb[par, k, pl.ds(0, rows), :], NT, preferred_element_type=jnp.float32)
        lse_tile = qb[par, k, pl.ds(rows + 16 * tiles, 16), :].astype(jnp.float32)
        biases = []
        block = lax.broadcasted_iota(jnp.int32, (per_shard, 128), 0)
        for t in range(tiles):
            rel = qb[par, k, pl.ds(rows + 16 * t, 16), :].astype(jnp.float32).astype(jnp.int32) - own * per_shard
            bits = jnp.where((rel >= 0) & (rel < per_shard), jnp.left_shift(1, jnp.maximum(jnp.minimum(rel, per_shard), 0)), 0)
            bits = jnp.sum(bits, axis=0, keepdims=True)
            named = jnp.right_shift(jnp.broadcast_to(bits, (per_shard, 128)), block) & 1
            biases.append(jnp.where(named == 1, jnp.broadcast_to(lse_tile[t : t + 1, :] * -LOG2E, (per_shard, 128)), -1e30))
        bias = jnp.concatenate(biases, axis=1)
        for b in range(per_shard):
            pt[par, k, pl.ds(b * BLK, BLK), :] = jnp.exp2(
                s[b * BLK : (b + 1) * BLK, :] * (scale * LOG2E) + bias[b : b + 1, :]
            )

    def grads(par, k):
        g = gb[par, k, pl.ds(0, rows), :]
        delta = row_of_tiles(gb[par, k, pl.ds(rows, 16), :].astype(jnp.float32))
        dp = lax.dot_general(vx[...], g, NT, preferred_element_type=jnp.float32)
        p = pt[par, k]
        ds = (p * (dp - delta)).astype(jnp.bfloat16)
        dv_acc[...] += jnp.dot(p.astype(jnp.bfloat16), g, preferred_element_type=jnp.float32)
        dk_acc[...] += jnp.dot(ds, qb[par, k, pl.ds(0, rows), :], preferred_element_type=jnp.float32)
        part[par, k] = jnp.dot(kt[...], ds, preferred_element_type=jnp.float32)

        @pl.when(par == 1)
        def _():
            give(k).start()

    def give(k):
        return pltpu.make_async_remote_copy(
            src_ref=part.at[1, k],
            dst_ref=pr.at[k],
            send_sem=p_send.at[k],
            recv_sem=p_recv.at[k],
            device_id=sib,
        )

    def gather_grad():
        pltpu.make_async_copy(rcv, rcv, a2a_recv).wait()
        both = rcv[...].astype(jnp.float32)
        g = both[:, 0:r, :].reshape(rows, dh)
        o = both[:, r : 2 * r, :].reshape(rows, dh)
        delta = lax.dot_general(
            jnp.ones((8, dh), jnp.float32), g * o, NT,
            precision=lax.Precision.HIGHEST, preferred_element_type=jnp.float32,
        )
        gb[0, 0, pl.ds(0, rows), :] = g.astype(jnp.bfloat16)
        gb[0, 0, pl.ds(rows, 16), :] = lane_tiles(delta[0:1, :])
        start_own(*g_ring)

    def q_step(d, _):
        relay(*q_ring, d)

        @pl.when(d == 2)
        def _():
            gather_grad()

        visit(d, q_ssend, q_srecv, qb, probs)
        return 0

    lax.fori_loop(0, 5, q_step, 0)

    def chain(side, d, h):
        return pltpu.make_async_remote_copy(
            src_ref=sl.at[side, d, h],
            dst_ref=rl.at[side, d - 1, h],
            send_sem=c_send.at[side, d, h],
            recv_sem=c_recv.at[side, d - 1, h],
            device_id=dirs[1 - side],
        )

    def local_sum(k, h):
        return part[0, k, pl.ds(h * half, half), :] + pr[k, pl.ds(h * half, half), :]

    def send_home(side, d, h, first):
        total = local_sum(slot(side, d), h)
        if not first:
            chain(side, d + 1, h).wait_recv()
            total = total + rl[side, d, h].astype(jnp.float32)
        sl[side, d, h] = total.astype(jnp.bfloat16)
        chain(side, d, h).start()

    def g_step(d, _):
        @pl.when(d == 4)
        def _():
            for k in (3, 5):
                give(k).wait_recv()
            send_home(0, 3, 1, True)
            send_home(1, 3, 0, True)

        relay(*g_ring, d)
        visit(d, g_ssend, g_srecv, gb, grads)
        return 0

    lax.fori_loop(0, 5, g_step, 0)

    for k in (0, 1, 2, 4, 6, 7):
        give(k).wait_recv()
    send_home(0, 4, 0, True)
    send_home(1, 4, 1, True)

    dk_v[...] = (dk_acc[...] * scale).astype(jnp.bfloat16)
    dv_v[...] = dv_acc[...].astype(jnp.bfloat16)
    stores = [
        pltpu.make_async_copy(dk_v, dk_hbm, out_sem.at[0]),
        pltpu.make_async_copy(dv_v, dv_hbm, out_sem.at[1]),
    ]
    for store in stores:
        store.start()

    for d in (2, 1):
        send_home(0, d, 1, False)
        send_home(1, d, 0, False)
        send_home(0, d + 1, 0, False)
        send_home(1, d + 1, 1, False)
    send_home(0, 1, 0, False)
    send_home(1, 1, 1, False)
    for h in range(2):
        total = local_sum(0, h)
        for side in range(2):
            chain(side, 1, h).wait_recv()
            total = total + rl[side, 0, h].astype(jnp.float32)
        dq_v[:, pl.ds(h * half, half)] = (total * scale).T.astype(jnp.bfloat16)
    stores.append(pltpu.make_async_copy(dq_v, dq_hbm, out_sem.at[2]))
    stores[2].start()

    drain(*q_ring)
    drain(*g_ring)

    def given(k, _):
        give(k).wait_send()
        return 0

    lax.fori_loop(0, RING, given, 0)
    for side in range(2):
        for d in range(1, 5):
            for h in range(2):
                if d < 4 or h == side:
                    chain(side, d, h).wait_send()
    if n_head > 1:
        others = msg.at[pl.ds(0, n_head - 1)]
        pltpu.make_async_copy(others, others, a2a_send).wait()
    for store in stores:
        store.wait()


def local(query_rows, key_rows, value_rows, attn_out, out_grad, logsumexp, shard_pick, block_pick):
    n_head = lax.axis_size("head")
    rows, dh = query_rows.shape
    keys = key_rows.shape[0]
    r = rows // n_head
    tiles = rows // 128
    q_rows = rows + 16 * tiles + 16
    g_rows = rows + 16
    groups, per_group = block_pick.shape[2:]
    bf, f32 = jnp.bfloat16, jnp.float32
    dma = pltpu.SemaphoreType.DMA
    vm = pltpu.VMEM
    return pl.pallas_call(
        functools.partial(kernel, n_head),
        out_shape=(
            jax.ShapeDtypeStruct((rows, dh), bf),
            jax.ShapeDtypeStruct((keys, dh), bf),
            jax.ShapeDtypeStruct((keys, dh), bf),
        ),
        in_specs=[pl.BlockSpec(memory_space=pl.ANY)] * 8,
        out_specs=(pl.BlockSpec(memory_space=pl.ANY),) * 3,
        scratch_shapes=[
            vm((2, RING, q_rows, dh), bf),
            vm((2, RING, g_rows, dh), bf),
            vm((keys, dh), bf),
            vm((keys, dh), bf),
            vm((dh, keys), bf),
            vm((r, n_head * dh), bf),
            vm((r, n_head * dh), bf),
            vm((1, rows), bf),
            vm((groups, rows), jnp.int32),
            vm((groups, per_group, rows), jnp.int32),
            vm((n_head, 2 * r, dh), bf),
            vm((n_head, 2 * r, dh), bf),
            vm((2, RING, keys, rows), f32),
            vm((2, RING, dh, rows), f32),
            vm((RING, dh, rows), f32),
            vm((2, 5, 2, dh // 2, rows), bf),
            vm((2, 4, 2, dh // 2, rows), bf),
            vm((keys, dh), f32),
            vm((keys, dh), f32),
            vm((rows, dh), bf),
            vm((keys, dh), bf),
            vm((keys, dh), bf),
            dma((8,)),
            dma,
            dma,
            dma((2, 4, 2)), dma((2, 5, 2)), dma((RING,)), dma((RING,)),
            dma((2, 4, 2)), dma((2, 5, 2)), dma((RING,)), dma((RING,)),
            dma((RING,)), dma((RING,)), dma((2, 5, 2)), dma((2, 4, 2)),
            dma((3,)),
        ],
        compiler_params=pltpu.CompilerParams(
            collective_id=0, has_side_effects=True, vmem_limit_bytes=56 << 20
        ),
        name="sparse_bwd",
    )(
        query_rows, key_rows, value_rows, attn_out, out_grad, logsumexp,
        shard_pick[0].T, block_pick[0].transpose(1, 2, 0),
    )


def solution(mesh):
    placed = (
        P("seq", "head"),
        P("seq", "head"),
        P("seq", "head"),
        P(("seq", "head"), None),
        P(("seq", "head"), None),
        P("head", "seq"),
        P("head", "seq", None),
        P("head", "seq", None, None),
    )
    return jax.shard_map(
        local,
        mesh=mesh,
        in_specs=placed,
        out_specs=(P("seq", "head"), P("seq", "head"), P("seq", "head")),
        check_vma=False,
    )
```

time: 180 us -> 73.1 us (0.41)
  waiting for transfers between devices: 104 us -> 0 us
  Pallas kernels: 0 us -> 67.8 us
  starting transfers between devices: 42 us -> 0 us
  matrix products: 24.3 us -> 0 us
  other arithmetic: 4.08 us -> 0 us
    all_to_all x5 -> x0, waiting for transfers between devices: 104 us -> none  [the longest x1 37.7 us: local(): lax.all_to_all(send_rows, 'seq', split_axis=0, concat_axis=0, tiled=True)]
    pallas_call x0 -> x1, Pallas kernels: none -> 67.8 us  [local(): pl.pallas_call(functools.partial(kernel, n_head), out_shape=(jax.ShapeDty...]
    all_to_all x5 -> x0, starting transfers between devices: 42 us -> none  [the longest x1 18.9 us: local(): lax.all_to_all(attn_out, 'head', split_axis=1, concat_axis=0, tiled=True)]
    dot_general x24 -> x0, matrix products: 24.3 us -> none  [the longest x1 8.13 us: local(): jnp.einsum('scr,scd->rd', dispatch, returned, precision=lax.Precision.HIG...]
    unnamed x7, local copies, waits for them, and re-layouts: 0.03 us -> 3.18 us
    convert_element_type x9 -> x0, other arithmetic: 2.81 us -> none  [the longest x1 0.74 us: local(): picks.astype(jnp.bfloat16)]
    reshape x5 -> x0, local copies, waits for them, and re-layouts: 2.13 us -> none  [the longest x4 1.92 us: block_terms(): jnp.broadcast_to(chosen[:, :, None], (count, per_shard, BLK))]
  transfers between devices with their start and end apart: 5 -> 0, of which waited for: 5 -> 0; matrix products, arithmetic and copies ran while one was open for 3% -> 0% of each run, Pallas kernels for 0% -> 0%
where the time goes in v1:
time: 73.1 us; the launch traced here: 71.7 us
  Pallas kernels  67.8 us (93%)
  local copies, waits for them, and re-layouts  3.18 us (4%)
    pallas_call x1, Pallas kernels, local(): pl.pallas_call(functools.partial(kernel, n_head), out_shape=(jax.ShapeDty...  67.8 us
    unnamed x7, local copies, waits for them, and re-layouts  3.18 us

profile of v1, /device:TPU:1, one launch (start us, length us, event | category | flops | bytes accessed | tf_op | source)
XLA Modules:
  0.0 71.7 jit_solution(5973546959202550615)
XLA Ops:
  0.6 67.8 %sparse_bwd.1 = (bf16[384,128]{1,0:T(8,128)(2,1)}, bf16[512,128]{1,0:T(8,128)(2,1)}, bf16[512,128]{1,0:T(8,128)(2,1)}) custom-call(bf16[384,128]{1,0:T(8,128)(2,1)} %q_hbm.1, bf16[512,128]{1,0:T(8,128)(2,1)} %k_hbm.1, bf16[512,128]{1,0:T(8,128)(2,1)} %v_hbm.1, bf16[8,6144]{1,0:T(8,128)(2,1)} %o_hbm.1, bf16[8,6144]{1,0:T(8,128)(2,1)} %g_hbm.1, ...), custom_call_target="tpu_custom_call" | custom-call | tf_op jit(solution)/shard_map/sparse_bwd/pallas_call | solution.py:374
  68.5 0.0 copy-start.1
  68.5 1.6 %copy.14 = bf16[384,128]{1,0:T(8,128)(2,1)} copy(bf16[384,128]{1,0:T(8,128)(2,1)} %get-tuple-element.6) | data formatting | bytes 196608
  70.1 0.0 copy-done.1
  70.1 0.0 copy-start
  70.1 0.7 copy.15
  70.7 0.3 copy-done
  71.0 0.7 copy.16
Async XLA Ops:
  68.5 1.6 %copy-start.1 = (bf16[512,128]{1,0:T(8,128)(2,1)S(1)}, bf16[512,128]{1,0:T(8,128)(2,1)}, u32[]{:S(2)}) copy-start(bf16[512,128]{1,0:T(8,128)(2,1)} %get-tuple-element.7) | copy-start | bytes 393220
  70.1 1.0 %copy-start = (bf16[512,128]{1,0:T(8,128)(2,1)S(1)}, bf16[512,128]{1,0:T(8,128)(2,1)}, u32[]{:S(2)}) copy-start(bf16[512,128]{1,0:T(8,128)(2,1)} %get-tuple-element.8) | copy-start | bytes 393220

commit v2 on v1

v2 whole, which is shorter than its diff:
```python
import functools
import math

import jax
import jax.numpy as jnp
from jax import lax
from jax.experimental import pallas as pl
from jax.experimental.pallas import tpu as pltpu
from jax.sharding import PartitionSpec as P

BLK = 64
RING = 8
HEAD_Z = 12
PIECES = 2
CHAIN = 4
LOG2E = math.log2(math.e)
NT = (((1,), (1,)), ((), ()))


def kernel(
    n_head, q_hbm, k_hbm, v_hbm, o_hbm, g_hbm, lse_hbm, sp_hbm, bp_hbm,
    dq_hbm, dk_hbm, dv_hbm,
    qb, gb, db, kx, vx, kt, o_v, g_v, lse_v, sp_v, bp_v, got_g, got_o,
    pt, part, pr, sl, rl, far_s, far_r, dk_acc, dv_acc, dq_v, dk_v, dv_v,
    in_sem, ga_send, ga_recv, oa_send, oa_recv,
    q_send, q_recv, q_ssend, q_srecv,
    g_send, g_recv, g_ssend, g_srecv,
    d_send, d_recv, d_ssend, d_srecv,
    p_send, p_recv, c_send, c_recv, f_send, f_recv, out_sem,
):
    rows, dh = q_hbm.shape
    tiles = rows // 128
    per_shard = kx.shape[0] // BLK
    r = rows // n_head
    own = lax.axis_index("seq")
    head = lax.axis_index("head")
    chip, core = own // 2, own % 2

    def at_chip(offset):
        return {"seq": ((chip + offset + RING) % RING) * 2 + core}

    right, left = at_chip(1), at_chip(-1)
    sib = {"seq": chip * 2 + (1 - core)}
    dirs = (right, left)
    far_home = (at_chip(-3), at_chip(3))
    scale = dh ** (-0.5)

    zn = HEAD_Z if n_head % HEAD_Z == 0 else n_head
    xn = n_head // zn

    my_x, my_z = head // zn, head % zn

    def away(n, i):
        m = (i + 1) // 2
        return (n // 2 + (2 * (i % 2) - 1) * m + n) % n

    def moved(at, by, n):
        if by == 0:
            return at
        at = at + by
        return jnp.where(at >= n, at - n, at)

    peer_z = [moved(my_z, away(zn, i), zn) for i in range(zn)]
    peer_x = [moved(my_x, away(xn, i), xn) * zn for i in range(xn)]
    peers = [x + z for z in peer_z for x in peer_x][: n_head - 1]

    barrier = pltpu.get_barrier_semaphore()
    for peer in peers:
        pl.semaphore_signal(barrier, inc=1, device_id={"head": peer})
    for peer in (right, left, sib) + far_home:
        pl.semaphore_signal(barrier, inc=1, device_id=peer)

    loads = [
        pltpu.make_async_copy(src, dst, in_sem.at[i])
        for i, (src, dst) in enumerate(
            (
                (q_hbm, qb.at[0, 0, pl.ds(0, rows)]),
                (lse_hbm, lse_v),
                (sp_hbm, sp_v),
                (bp_hbm, bp_v),
                (g_hbm, g_v),
                (o_hbm, o_v),
                (k_hbm, kx),
                (v_hbm, vx),
            )
        )
    ]
    for load in loads:
        load.start()

    for load in loads[:4]:
        load.wait()

    lse = lse_v[...].astype(jnp.float32)
    for t in range(tiles):
        cols = pl.ds(t * 128, 128)
        ids = [sp_v[g : g + 1, cols] * per_shard + bp_v[g, :, cols] for g in range(sp_v.shape[0])]
        ids = jnp.concatenate(ids, axis=0).astype(jnp.float32).astype(jnp.bfloat16)
        qb[0, 0, pl.ds(rows + 16 * t, 16), :] = ids
    sub = lax.broadcasted_iota(jnp.int32, (16, 128), 0)

    def lane_tiles(vec):
        out = jnp.broadcast_to(vec[:, 0:128], (16, 128))
        for t in range(1, tiles):
            out = jnp.where(sub == t, jnp.broadcast_to(vec[:, t * 128 : (t + 1) * 128], (16, 128)), out)
        return out.astype(jnp.bfloat16)

    qb[0, 0, pl.ds(rows + 16 * tiles, 16), :] = lane_tiles(lse)
    for load in loads[4:6]:
        load.wait()

    def slot(side, d):
        return d if side == 0 else (RING - d) % RING

    class Ring:
        def __init__(self, buf, pieces, send, recv, ssend, srecv):
            self.buf, self.pieces = buf, pieces
            self.send, self.recv, self.ssend, self.srecv = send, recv, ssend, srecv
            self.size = buf.shape[2] // pieces

        def hop(self, side, d, h):
            span = pl.ds(pl.multiple_of(h * self.size, 8), self.size)
            return pltpu.make_async_remote_copy(
                src_ref=self.buf.at[0, slot(side, d), span],
                dst_ref=self.buf.at[0, slot(side, d + 1), span],
                send_sem=self.send.at[side, d, h],
                recv_sem=self.recv.at[side, d + 1, h],
                device_id=dirs[side],
            )

        def twin(self, k):
            return pltpu.make_async_remote_copy(
                src_ref=self.buf.at[0, k],
                dst_ref=self.buf.at[1, k],
                send_sem=self.ssend.at[k],
                recv_sem=self.srecv.at[k],
                device_id=sib,
            )

        def order(self, side, i):
            return (i + side * (self.pieces // 2)) % self.pieces

        def last_hop(self, side, i):
            return i < self.pieces // 2 if self.pieces > 1 else side == 0

        def start_own(self):
            for i in range(self.pieces):
                for side in range(2):
                    self.hop(side, 0, self.order(side, i)).start()
            self.twin(0).start()

        def relay(self, d):
            def one(i, _):
                self.relay_piece(d, i)
                return 0

            lax.fori_loop(0, self.pieces, one, 0)
            self.twin(d).start()

            @pl.when(d < 4)
            def _():
                self.twin(RING - d).start()

        def relay_piece(self, d, i):
            for side in range(2):
                h = self.order(side, i)

                @pl.when((d < 4) | self.last_hop(side, i))
                def _():
                    self.hop(side, d - 1, h).wait_recv()

                @pl.when((d < 3) | ((d == 3) & self.last_hop(side, i)))
                def _():
                    self.hop(side, d, h).start()

        def drain(self):
            def per_hop(d, _):
                def per_piece(i, _):
                    for side in range(2):
                        @pl.when((d < 3) | self.last_hop(side, i))
                        def _():
                            self.hop(side, d, self.order(side, i)).wait_send()
                    return 0

                return lax.fori_loop(0, self.pieces, per_piece, 0)

            lax.fori_loop(0, 4, per_hop, 0)

            def per_slot(k, _):
                self.twin(k).wait_send()
                return 0

            lax.fori_loop(0, RING, per_slot, 0)

    q_ring = Ring(qb, PIECES, q_send, q_recv, q_ssend, q_srecv)
    g_ring = Ring(gb, PIECES, g_send, g_recv, g_ssend, g_srecv)
    d_ring = Ring(db, 1, d_send, d_recv, d_ssend, d_srecv)

    def to_head(src, dst, send, recv, some):
        for peer in some:
            pltpu.make_async_remote_copy(
                src_ref=src.at[:, pl.ds(pl.multiple_of(peer * dh, dh), dh)],
                dst_ref=dst.at[head],
                send_sem=send,
                recv_sem=recv,
                device_id={"head": peer},
            ).start()

    def to_self(src, dst, recv):
        mine = src.at[:, pl.ds(pl.multiple_of(head * dh, dh), dh)]
        pltpu.make_async_copy(mine, dst.at[head], recv).start()

    pl.semaphore_wait(barrier, n_head - 1 + 5)
    to_head(g_v, got_g, ga_send, ga_recv, peers)
    to_self(g_v, got_g, ga_recv)
    q_ring.start_own()
    to_head(o_v, got_o, oa_send, oa_recv, peers)
    to_self(o_v, got_o, oa_recv)

    for load in loads[6:]:
        load.wait()

    def probs(par, k):
        s = lax.dot_general(kx[...], qb[par, k, pl.ds(0, rows), :], NT, preferred_element_type=jnp.float32)
        lse_tile = qb[par, k, pl.ds(rows + 16 * tiles, 16), :].astype(jnp.float32)
        biases = []
        block = lax.broadcasted_iota(jnp.int32, (per_shard, 128), 0)
        for t in range(tiles):
            rel = qb[par, k, pl.ds(rows + 16 * t, 16), :].astype(jnp.float32).astype(jnp.int32) - own * per_shard
            bits = jnp.where((rel >= 0) & (rel < per_shard), jnp.left_shift(1, jnp.maximum(jnp.minimum(rel, per_shard), 0)), 0)
            bits = jnp.sum(bits, axis=0, keepdims=True)
            named = jnp.right_shift(jnp.broadcast_to(bits, (per_shard, 128)), block) & 1
            biases.append(jnp.where(named == 1, jnp.broadcast_to(lse_tile[t : t + 1, :] * -LOG2E, (per_shard, 128)), -1e30))
        bias = jnp.concatenate(biases, axis=1)
        for b in range(per_shard):
            pt[par, k, pl.ds(b * BLK, BLK), :] = jnp.exp2(
                s[b * BLK : (b + 1) * BLK, :] * (scale * LOG2E) + bias[b : b + 1, :]
            )

    def give(k):
        return pltpu.make_async_remote_copy(
            src_ref=part.at[1, k],
            dst_ref=pr.at[k],
            send_sem=p_send.at[k],
            recv_sem=p_recv.at[k],
            device_id=sib,
        )

    def grads(par, k):
        g = gb[par, k]
        tile = db[par, k].astype(jnp.float32)
        delta = jnp.concatenate([tile[t : t + 1, :] for t in range(tiles)], axis=1)
        dp = lax.dot_general(vx[...], g, NT, preferred_element_type=jnp.float32)
        p = pt[par, k]
        ds = (p * (dp - delta)).astype(jnp.bfloat16)
        part[par, k] = jnp.dot(kt[...], ds, preferred_element_type=jnp.float32)

        @pl.when(par == 1)
        def _():
            give(k).start()

        dv_acc[...] += jnp.dot(p.astype(jnp.bfloat16), g, preferred_element_type=jnp.float32)
        dk_acc[...] += jnp.dot(ds, qb[par, k, pl.ds(0, rows), :], preferred_element_type=jnp.float32)

    def visit(d, par, side, rings, compute):
        k = jnp.where(side == 0, d, (RING - d) % RING)

        @pl.when(((side == 0) & (d >= 0) & (d <= 4)) | ((d >= 1) & (d < 4)))
        def _():
            @pl.when(par == 1)
            def _():
                for ring in rings:
                    ring.twin(k).wait_recv()

            compute(par, k)

    width = dh // CHAIN

    def chain(side, d, h):
        return pltpu.make_async_remote_copy(
            src_ref=sl.at[side, d, h],
            dst_ref=rl.at[side, d - 1, h],
            send_sem=c_send.at[side, d, h],
            recv_sem=c_recv.at[side, d - 1, h],
            device_id=dirs[1 - side],
        )

    def far(side):
        return pltpu.make_async_remote_copy(
            src_ref=far_s.at[side],
            dst_ref=far_r.at[side],
            send_sem=f_send.at[side],
            recv_sem=f_recv.at[side],
            device_id=far_home[side],
        )

    def local_sum(k, h):
        return part[0, k, pl.ds(h * width, width), :] + pr[k, pl.ds(h * width, width), :]

    def mine_to_take(side, h):
        return (h < CHAIN // 2) == (side == 0)

    def send_home(d):
        for side in range(2):
            give(slot(side, d)).wait_recv()
        for i in range(CHAIN):
            for side in range(2):
                h = (i + (1 - side) * (CHAIN // 2)) % CHAIN
                total = local_sum(slot(side, d), h)
                if d < 3:
                    chain(side, d + 1, h).wait_recv()
                    total = total + rl[side, d, h].astype(jnp.float32)
                if d == 1 and mine_to_take(side, h):
                    if i == CHAIN // 2:
                        far(side).wait_recv()
                    total = total + far_r[side, i - CHAIN // 2].astype(jnp.float32)
                sl[side, d, h] = total.astype(jnp.bfloat16)
                chain(side, d, h).start()

    def tick(t, _):
        @pl.when((t >= 1) & (t <= 4))
        def _():
            q_ring.relay(t)

        def forward(j, _):
            visit(t, j // 2, j % 2, (q_ring,), probs)
            return 0

        @pl.when(t <= 4)
        def _():
            lax.fori_loop(0, 4, forward, 0)

        @pl.when(t == 2)
        def _():
            pltpu.make_async_copy(got_g, got_g, ga_recv).wait()
            g = got_g[...].astype(jnp.float32).reshape(rows, dh)
            gb[0, 0] = g.astype(jnp.bfloat16)
            g_ring.start_own()
            kt[...] = kx[...].astype(jnp.float32).T.astype(jnp.bfloat16)
            dk_acc[...] = jnp.zeros_like(dk_acc)
            dv_acc[...] = jnp.zeros_like(dv_acc)
            pltpu.make_async_copy(got_o, got_o, oa_recv).wait()
            o = got_o[...].astype(jnp.float32).reshape(rows, dh)
            delta = lax.dot_general(
                jnp.ones((8, dh), jnp.float32), gb[0, 0].astype(jnp.float32) * o, NT,
                precision=lax.Precision.HIGHEST, preferred_element_type=jnp.float32,
            )
            db[0, 0] = lane_tiles(delta[0:1, :])
            d_ring.start_own()

        @pl.when(t >= 3)
        def _():
            g_ring.relay(t - 2)
            d_ring.relay(t - 2)

        def backward(j, _):
            visit(t - 2, j // 2, j % 2, (g_ring, d_ring), grads)

            @pl.when((t == 6) & (j == 1))
            def _():
                send_home(3)

            return 0

        @pl.when(t >= 2)
        def _():
            lax.fori_loop(0, 4, backward, 0)

        return 0

    lax.fori_loop(0, 7, tick, 0)

    give(4).wait_recv()
    for side in range(2):
        for i in range(CHAIN // 2):
            far_s[side, i] = local_sum(4, side * (CHAIN // 2) + i).astype(jnp.bfloat16)
        far(side).start()

    dk_v[...] = (dk_acc[...] * scale).astype(jnp.bfloat16)
    dv_v[...] = dv_acc[...].astype(jnp.bfloat16)
    stores = [
        pltpu.make_async_copy(dk_v, dk_hbm, out_sem.at[0]),
        pltpu.make_async_copy(dv_v, dv_hbm, out_sem.at[1]),
        pltpu.make_async_copy(dq_v, dq_hbm, out_sem.at[2]),
    ]
    stores[0].start()
    stores[1].start()

    send_home(2)
    send_home(1)
    give(0).wait_recv()
    totals = []
    for h in range(CHAIN):
        total = local_sum(0, h)
        for side in range(2):
            chain(side, 1, h).wait_recv()
            total = total + rl[side, 0, h].astype(jnp.float32)
        totals.append(total)
    dq_v[...] = (jnp.concatenate(totals, axis=0) * scale).T.astype(jnp.bfloat16)
    stores[2].start()

    q_ring.drain()
    g_ring.drain()
    d_ring.drain()

    def given(k, _):
        give(k).wait_send()
        return 0

    lax.fori_loop(0, RING, given, 0)
    for side in range(2):
        far(side).wait_send()
        for d in range(1, 4):
            for h in range(CHAIN):
                chain(side, d, h).wait_send()
    if n_head > 1:
        for got, sem in ((got_g, ga_send), (got_o, oa_send)):
            others = got.at[pl.ds(0, n_head - 1)]
            pltpu.make_async_copy(others, others, sem).wait()
    for store in stores:
        store.wait()


def local(query_rows, key_rows, value_rows, attn_out, out_grad, logsumexp, shard_pick, block_pick):
    n_head = lax.axis_size("head")
    rows, dh = query_rows.shape
    keys = key_rows.shape[0]
    r = rows // n_head
    tiles = rows // 128
    q_rows = rows + 16 * tiles + 16
    groups, per_group = block_pick.shape[2:]
    bf, f32 = jnp.bfloat16, jnp.float32
    dma = pltpu.SemaphoreType.DMA
    vm = pltpu.VMEM
    return pl.pallas_call(
        functools.partial(kernel, n_head),
        out_shape=(
            jax.ShapeDtypeStruct((rows, dh), bf),
            jax.ShapeDtypeStruct((keys, dh), bf),
            jax.ShapeDtypeStruct((keys, dh), bf),
        ),
        in_specs=[pl.BlockSpec(memory_space=pl.ANY)] * 8,
        out_specs=(pl.BlockSpec(memory_space=pl.ANY),) * 3,
        scratch_shapes=[
            vm((2, RING, q_rows, dh), bf),
            vm((2, RING, rows, dh), bf),
            vm((2, RING, 16, dh), bf),
            vm((keys, dh), bf),
            vm((keys, dh), bf),
            vm((dh, keys), bf),
            vm((r, n_head * dh), bf),
            vm((r, n_head * dh), bf),
            vm((1, rows), bf),
            vm((groups, rows), jnp.int32),
            vm((groups, per_group, rows), jnp.int32),
            vm((n_head, r, dh), bf),
            vm((n_head, r, dh), bf),
            vm((2, RING, keys, rows), f32),
            vm((2, RING, dh, rows), f32),
            vm((RING, dh, rows), f32),
            vm((2, 4, CHAIN, dh // CHAIN, rows), bf),
            vm((2, 3, CHAIN, dh // CHAIN, rows), bf),
            vm((2, CHAIN // 2, dh // CHAIN, rows), bf),
            vm((2, CHAIN // 2, dh // CHAIN, rows), bf),
            vm((keys, dh), f32),
            vm((keys, dh), f32),
            vm((rows, dh), bf),
            vm((keys, dh), bf),
            vm((keys, dh), bf),
            dma((8,)),
            dma, dma, dma, dma,
            dma((2, 4, PIECES)), dma((2, 5, PIECES)), dma((RING,)), dma((RING,)),
            dma((2, 4, PIECES)), dma((2, 5, PIECES)), dma((RING,)), dma((RING,)),
            dma((2, 4, 1)), dma((2, 5, 1)), dma((RING,)), dma((RING,)),
            dma((RING,)), dma((RING,)), dma((2, 4, CHAIN)), dma((2, 3, CHAIN)),
            dma((2,)), dma((2,)), dma((3,)),
        ],
        compiler_params=pltpu.CompilerParams(
            collective_id=0, has_side_effects=True, vmem_limit_bytes=56 << 20
        ),
        name="sparse_bwd",
    )(
        query_rows, key_rows, value_rows, attn_out, out_grad, logsumexp,
        shard_pick[0].T, block_pick[0].transpose(1, 2, 0),
    )


def solution(mesh):
    placed = (
        P("seq", "head"),
        P("seq", "head"),
        P("seq", "head"),
        P(("seq", "head"), None),
        P(("seq", "head"), None),
        P("head", "seq"),
        P("head", "seq", None),
        P("head", "seq", None, None),
    )
    return jax.shard_map(
        local,
        mesh=mesh,
        in_specs=placed,
        out_specs=(P("seq", "head"), P("seq", "head"), P("seq", "head")),
        check_vma=False,
    )
```

time: 73.1 us -> 68.2 us (0.933); the launches traced: 71.7 us -> 68 us
  Pallas kernels: 67.8 us -> 64.2 us
    pallas_call x1, Pallas kernels: 67.8 us -> 64.2 us  [local(): pl.pallas_call(functools.partial(kernel, n_head), out_shape=(jax.ShapeDty...]
where the time goes in v2:
time: 68.2 us; the launch traced here: 68 us
  Pallas kernels  64.2 us (94%)
  local copies, waits for them, and re-layouts  3.18 us (5%)
    pallas_call x1, Pallas kernels, local(): pl.pallas_call(functools.partial(kernel, n_head), out_shape=(jax.ShapeDty...  64.2 us
    unnamed x7, local copies, waits for them, and re-layouts  3.18 us

profile of v2, /device:TPU:1, one launch (start us, length us, event | category | flops | bytes accessed | tf_op | source)
XLA Modules:
  0.0 68.0 jit_solution(17056974737576168786)
XLA Ops:
  0.6 64.2 %sparse_bwd.1 = (bf16[384,128]{1,0:T(8,128)(2,1)}, bf16[512,128]{1,0:T(8,128)(2,1)}, bf16[512,128]{1,0:T(8,128)(2,1)}) custom-call(bf16[384,128]{1,0:T(8,128)(2,1)} %q_hbm.1, bf16[512,128]{1,0:T(8,128)(2,1)} %k_hbm.1, bf16[512,128]{1,0:T(8,128)(2,1)} %v_hbm.1, bf16[8,6144]{1,0:T(8,128)(2,1)} %o_hbm.1, bf16[8,6144]{1,0:T(8,128)(2,1)} %g_hbm.1, ...), custom_call_target="tpu_custom_call" | custom-call | tf_op jit(solution)/shard_map/sparse_bwd/pallas_call | solution.py:435
  64.8 0.0 copy-start.1
  64.8 1.6 %copy.14 = bf16[384,128]{1,0:T(8,128)(2,1)} copy(bf16[384,128]{1,0:T(8,128)(2,1)} %get-tuple-element.6) | data formatting | bytes 196608
  66.4 0.0 copy-done.1
  66.4 0.0 copy-start
  66.4 0.7 copy.15
  67.1 0.3 copy-done
  67.4 0.7 copy.16
Async XLA Ops:
  64.8 1.6 %copy-start.1 = (bf16[512,128]{1,0:T(8,128)(2,1)S(1)}, bf16[512,128]{1,0:T(8,128)(2,1)}, u32[]{:S(2)}) copy-start(bf16[512,128]{1,0:T(8,128)(2,1)} %get-tuple-element.7) | copy-start | bytes 393220
  66.4 1.0 %copy-start = (bf16[512,128]{1,0:T(8,128)(2,1)S(1)}, bf16[512,128]{1,0:T(8,128)(2,1)}, u32[]{:S(2)}) copy-start(bf16[512,128]{1,0:T(8,128)(2,1)} %get-tuple-element.8) | copy-start | bytes 393220

commit v3 on v2

--- a/solution.py
+++ b/solution.py
@@ -11,7 +11,6 @@
 BLK = 64
 RING = 8
 HEAD_Z = 12
-PIECES = 2
 CHAIN = 4
 LOG2E = math.log2(math.e)
 NT = (((1,), (1,)), ((), ()))
@@ -20,12 +19,11 @@
 def kernel(
     n_head, q_hbm, k_hbm, v_hbm, o_hbm, g_hbm, lse_hbm, sp_hbm, bp_hbm,
     dq_hbm, dk_hbm, dv_hbm,
-    qb, gb, db, kx, vx, kt, o_v, g_v, lse_v, sp_v, bp_v, got_g, got_o,
+    qb, gb, kx, vx, kt, o_v, g_v, lse_v, sp_v, bp_v, got_g, got_o,
     pt, part, pr, sl, rl, far_s, far_r, dk_acc, dv_acc, dq_v, dk_v, dv_v,
     in_sem, ga_send, ga_recv, oa_send, oa_recv,
     q_send, q_recv, q_ssend, q_srecv,
     g_send, g_recv, g_ssend, g_srecv,
-    d_send, d_recv, d_ssend, d_srecv,
     p_send, p_recv, c_send, c_recv, f_send, f_recv, out_sem,
 ):
     rows, dh = q_hbm.shape
@@ -113,16 +111,15 @@
         return d if side == 0 else (RING - d) % RING
 
     class Ring:
-        def __init__(self, buf, pieces, send, recv, ssend, srecv):
-            self.buf, self.pieces = buf, pieces
+        def __init__(self, buf, cut, send, recv, ssend, srecv):
+            self.buf = buf
+            self.spans = (pl.ds(0, cut), pl.ds(cut, buf.shape[2] - cut))
             self.send, self.recv, self.ssend, self.srecv = send, recv, ssend, srecv
-            self.size = buf.shape[2] // pieces
 
         def hop(self, side, d, h):
-            span = pl.ds(pl.multiple_of(h * self.size, 8), self.size)
             return pltpu.make_async_remote_copy(
-                src_ref=self.buf.at[0, slot(side, d), span],
-                dst_ref=self.buf.at[0, slot(side, d + 1), span],
+                src_ref=self.buf.at[0, slot(side, d), self.spans[h]],
+                dst_ref=self.buf.at[0, slot(side, d + 1), self.spans[h]],
                 send_sem=self.send.at[side, d, h],
                 recv_sem=self.recv.at[side, d + 1, h],
                 device_id=dirs[side],
@@ -137,52 +134,35 @@
                 device_id=sib,
             )
 
-        def order(self, side, i):
-            return (i + side * (self.pieces // 2)) % self.pieces
-
-        def last_hop(self, side, i):
-            return i < self.pieces // 2 if self.pieces > 1 else side == 0
-
-        def start_own(self):
-            for i in range(self.pieces):
+        def start_piece(self, h):
+            for side in range(2):
+                self.hop(side, 0, h).start()
+
+        def relay(self, d):
+            for h in range(2):
                 for side in range(2):
-                    self.hop(side, 0, self.order(side, i)).start()
-            self.twin(0).start()
-
-        def relay(self, d):
-            def one(i, _):
-                self.relay_piece(d, i)
-                return 0
-
-            lax.fori_loop(0, self.pieces, one, 0)
+                    @pl.when((d < 4) | (h == side))
+                    def _():
+                        self.hop(side, d - 1, h).wait_recv()
+
+                    @pl.when((d < 3) | ((d == 3) & (h == side)))
+                    def _():
+                        self.hop(side, d, h).start()
+
             self.twin(d).start()
 
             @pl.when(d < 4)
             def _():
                 self.twin(RING - d).start()
 
-        def relay_piece(self, d, i):
-            for side in range(2):
-                h = self.order(side, i)
-
-                @pl.when((d < 4) | self.last_hop(side, i))
-                def _():
-                    self.hop(side, d - 1, h).wait_recv()
-
-                @pl.when((d < 3) | ((d == 3) & self.last_hop(side, i)))
-                def _():
-                    self.hop(side, d, h).start()
-
         def drain(self):
             def per_hop(d, _):
-                def per_piece(i, _):
+                for h in range(2):
                     for side in range(2):
-                        @pl.when((d < 3) | self.last_hop(side, i))
+                        @pl.when((d < 3) | (h == side))
                         def _():
-                            self.hop(side, d, self.order(side, i)).wait_send()
-                    return 0
-
-                return lax.fori_loop(0, self.pieces, per_piece, 0)
+                            self.hop(side, d, h).wait_send()
+                return 0
 
             lax.fori_loop(0, 4, per_hop, 0)
 
@@ -192,9 +172,8 @@
 
             lax.fori_loop(0, RING, per_slot, 0)
 
-    q_ring = Ring(qb, PIECES, q_send, q_recv, q_ssend, q_srecv)
-    g_ring = Ring(gb, PIECES, g_send, g_recv, g_ssend, g_srecv)
-    d_ring = Ring(db, 1, d_send, d_recv, d_ssend, d_srecv)
+    q_ring = Ring(qb, qb.shape[2] // 2, q_send, q_recv, q_ssend, q_srecv)
+    g_ring = Ring(gb, rows // 2, g_send, g_recv, g_ssend, g_srecv)
 
     def to_head(src, dst, send, recv, some):
         for peer in some:
@@ -213,7 +192,9 @@
     pl.semaphore_wait(barrier, n_head - 1 + 5)
     to_head(g_v, got_g, ga_send, ga_recv, peers)
     to_self(g_v, got_g, ga_recv)
-    q_ring.start_own()
+    q_ring.start_piece(0)
+    q_ring.start_piece(1)
+    q_ring.twin(0).start()
     to_head(o_v, got_o, oa_send, oa_recv, peers)
     to_self(o_v, got_o, oa_recv)
 
@@ -246,21 +227,44 @@
             device_id=sib,
         )
 
-    def grads(par, k):
-        g = gb[par, k]
-        tile = db[par, k].astype(jnp.float32)
+    def score_grads(par, k):
+        g = gb[par, k, pl.ds(0, rows), :]
+        tile = gb[par, k, pl.ds(rows, 16), :].astype(jnp.float32)
         delta = jnp.concatenate([tile[t : t + 1, :] for t in range(tiles)], axis=1)
         dp = lax.dot_general(vx[...], g, NT, preferred_element_type=jnp.float32)
         p = pt[par, k]
         ds = (p * (dp - delta)).astype(jnp.bfloat16)
         part[par, k] = jnp.dot(kt[...], ds, preferred_element_type=jnp.float32)
-
-        @pl.when(par == 1)
-        def _():
-            give(k).start()
-
-        dv_acc[...] += jnp.dot(p.astype(jnp.bfloat16), g, preferred_element_type=jnp.float32)
-        dk_acc[...] += jnp.dot(ds, qb[par, k, pl.ds(0, rows), :], preferred_element_type=jnp.float32)
+        return p.astype(jnp.bfloat16), g, ds, qb[par, k, pl.ds(0, rows), :]
+
+    def grads(first, second):
+        p, g, ds, q = (jnp.concatenate(both, axis=i) for both, i in zip(zip(score_grads(*first), score_grads(*second)), (1, 0, 1, 0)))
+        dv_acc[...] += jnp.dot(p, g, preferred_element_type=jnp.float32)
+        dk_acc[...] += jnp.dot(ds, q, preferred_element_type=jnp.float32)
+
+    def backward_pair(d, par):
+        single = (d == 0) | (d == 4)
+        par1 = jnp.where(single, 0, par)
+        par2 = jnp.where(single, 1, par)
+        k2 = jnp.where(single, d, RING - d)
+
+        @pl.when(par1 == 1)
+        def _():
+            g_ring.twin(d).wait_recv()
+
+        @pl.when(par2 == 1)
+        def _():
+            g_ring.twin(k2).wait_recv()
+
+        grads((par1, d), (par2, k2))
+
+        @pl.when(par1 == 1)
+        def _():
+            give(d).start()
+
+        @pl.when(par2 == 1)
+        def _():
+            give(k2).start()
 
     def visit(d, par, side, rings, compute):
         k = jnp.where(side == 0, d, (RING - d) % RING)
@@ -334,37 +338,36 @@
         def _():
             pltpu.make_async_copy(got_g, got_g, ga_recv).wait()
             g = got_g[...].astype(jnp.float32).reshape(rows, dh)
-            gb[0, 0] = g.astype(jnp.bfloat16)
-            g_ring.start_own()
+            gb[0, 0, pl.ds(0, rows), :] = g.astype(jnp.bfloat16)
+            g_ring.start_piece(0)
             kt[...] = kx[...].astype(jnp.float32).T.astype(jnp.bfloat16)
             dk_acc[...] = jnp.zeros_like(dk_acc)
             dv_acc[...] = jnp.zeros_like(dv_acc)
             pltpu.make_async_copy(got_o, got_o, oa_recv).wait()
             o = got_o[...].astype(jnp.float32).reshape(rows, dh)
             delta = lax.dot_general(
-                jnp.ones((8, dh), jnp.float32), gb[0, 0].astype(jnp.float32) * o, NT,
+                jnp.ones((8, dh), jnp.float32), gb[0, 0, pl.ds(0, rows), :].astype(jnp.float32) * o, NT,
                 precision=lax.Precision.HIGHEST, preferred_element_type=jnp.float32,
             )
-            db[0, 0] = lane_tiles(delta[0:1, :])
-            d_ring.start_own()
+            gb[0, 0, pl.ds(rows, 16), :] = lane_tiles(delta[0:1, :])
+            g_ring.start_piece(1)
+            g_ring.twin(0).start()
 
         @pl.when(t >= 3)
         def _():
             g_ring.relay(t - 2)
-            d_ring.relay(t - 2)
 
         def backward(j, _):
-            visit(t - 2, j // 2, j % 2, (g_ring, d_ring), grads)
-
-            @pl.when((t == 6) & (j == 1))
-            def _():
-                send_home(3)
-
+            backward_pair(t - 2, j)
             return 0
 
+        @pl.when(t == 6)
+        def _():
+            send_home(3)
+
         @pl.when(t >= 2)
         def _():
-            lax.fori_loop(0, 4, backward, 0)
+            lax.fori_loop(0, jnp.where((t == 2) | (t == 6), 1, 2), backward, 0)
 
         return 0
 
@@ -401,7 +404,6 @@
 
     q_ring.drain()
     g_ring.drain()
-    d_ring.drain()
 
     def given(k, _):
         give(k).wait_send()
@@ -443,8 +445,7 @@
         out_specs=(pl.BlockSpec(memory_space=pl.ANY),) * 3,
         scratch_shapes=[
             vm((2, RING, q_rows, dh), bf),
-            vm((2, RING, rows, dh), bf),
-            vm((2, RING, 16, dh), bf),
+            vm((2, RING, rows + 16, dh), bf),
             vm((keys, dh), bf),
             vm((keys, dh), bf),
             vm((dh, keys), bf),
@@ -469,9 +470,8 @@
             vm((keys, dh), bf),
             dma((8,)),
             dma, dma, dma, dma,
-            dma((2, 4, PIECES)), dma((2, 5, PIECES)), dma((RING,)), dma((RING,)),
-            dma((2, 4, PIECES)), dma((2, 5, PIECES)), dma((RING,)), dma((RING,)),
-            dma((2, 4, 1)), dma((2, 5, 1)), dma((RING,)), dma((RING,)),
+            dma((2, 4, 2)), dma((2, 5, 2)), dma((RING,)), dma((RING,)),
+            dma((2, 4, 2)), dma((2, 5, 2)), dma((RING,)), dma((RING,)),
             dma((RING,)), dma((RING,)), dma((2, 4, CHAIN)), dma((2, 3, CHAIN)),
             dma((2,)), dma((2,)), dma((3,)),
         ],

time: 68.2 us -> 67.6 us (level)
  no operation moved by 1% of the time
where the time goes in v3:
time: 67.6 us; the launch traced here: 67.4 us
  Pallas kernels  63.6 us (94%)
  local copies, waits for them, and re-layouts  3.18 us (5%)
    pallas_call x1, Pallas kernels, local(): pl.pallas_call(functools.partial(kernel, n_head), out_shape=(jax.ShapeDty...  63.6 us
    unnamed x7, local copies, waits for them, and re-layouts  3.18 us

profile of v3, /device:TPU:1, one launch (start us, length us, event | category | flops | bytes accessed | tf_op | source)
XLA Modules:
  0.0 67.4 jit_solution(8954701072514652449)
XLA Ops:
  0.6 63.6 %sparse_bwd.1 = (bf16[384,128]{1,0:T(8,128)(2,1)}, bf16[512,128]{1,0:T(8,128)(2,1)}, bf16[512,128]{1,0:T(8,128)(2,1)}) custom-call(bf16[384,128]{1,0:T(8,128)(2,1)} %q_hbm.1, bf16[512,128]{1,0:T(8,128)(2,1)} %k_hbm.1, bf16[512,128]{1,0:T(8,128)(2,1)} %v_hbm.1, bf16[8,6144]{1,0:T(8,128)(2,1)} %o_hbm.1, bf16[8,6144]{1,0:T(8,128)(2,1)} %g_hbm.1, ...), custom_call_target="tpu_custom_call" | custom-call | tf_op jit(solution)/shard_map/sparse_bwd/pallas_call | solution.py:437
  64.2 0.0 copy-start.1
  64.3 1.6 %copy.14 = bf16[384,128]{1,0:T(8,128)(2,1)} copy(bf16[384,128]{1,0:T(8,128)(2,1)} %get-tuple-element.6) | data formatting | bytes 196608
  65.8 0.0 copy-done.1
  65.8 0.0 copy-start
  65.8 0.7 copy.15
  66.5 0.3 copy-done
  66.8 0.7 copy.16
Async XLA Ops:
  64.2 1.6 %copy-start.1 = (bf16[512,128]{1,0:T(8,128)(2,1)S(1)}, bf16[512,128]{1,0:T(8,128)(2,1)}, u32[]{:S(2)}) copy-start(bf16[512,128]{1,0:T(8,128)(2,1)} %get-tuple-element.7) | copy-start | bytes 393220
  65.8 1.0 %copy-start = (bf16[512,128]{1,0:T(8,128)(2,1)S(1)}, bf16[512,128]{1,0:T(8,128)(2,1)}, u32[]{:S(2)}) copy-start(bf16[512,128]{1,0:T(8,128)(2,1)} %get-tuple-element.8) | copy-start | bytes 393220

commit v4 on v3

--- a/solution.py
+++ b/solution.py
@@ -326,14 +326,6 @@
         def _():
             q_ring.relay(t)
 
-        def forward(j, _):
-            visit(t, j // 2, j % 2, (q_ring,), probs)
-            return 0
-
-        @pl.when(t <= 4)
-        def _():
-            lax.fori_loop(0, 4, forward, 0)
-
         @pl.when(t == 2)
         def _():
             pltpu.make_async_copy(got_g, got_g, ga_recv).wait()
@@ -343,6 +335,17 @@
             kt[...] = kx[...].astype(jnp.float32).T.astype(jnp.bfloat16)
             dk_acc[...] = jnp.zeros_like(dk_acc)
             dv_acc[...] = jnp.zeros_like(dv_acc)
+
+        def forward(j, _):
+            visit(t, j // 2, j % 2, (q_ring,), probs)
+            return 0
+
+        @pl.when(t <= 4)
+        def _():
+            lax.fori_loop(0, 4, forward, 0)
+
+        @pl.when(t == 2)
+        def _():
             pltpu.make_async_copy(got_o, got_o, oa_recv).wait()
             o = got_o[...].astype(jnp.float32).reshape(rows, dh)
             delta = lax.dot_general(
@@ -388,6 +391,19 @@
     ]
     stores[0].start()
     stores[1].start()
+
+    q_ring.drain()
+    g_ring.drain()
+
+    def given(k, _):
+        give(k).wait_send()
+        return 0
+
+    lax.fori_loop(0, RING, given, 0)
+    if n_head > 1:
+        for got, sem in ((got_g, ga_send), (got_o, oa_send)):
+            others = got.at[pl.ds(0, n_head - 1)]
+            pltpu.make_async_copy(others, others, sem).wait()
 
     send_home(2)
     send_home(1)
@@ -402,23 +418,11 @@
     dq_v[...] = (jnp.concatenate(totals, axis=0) * scale).T.astype(jnp.bfloat16)
     stores[2].start()
 
-    q_ring.drain()
-    g_ring.drain()
-
-    def given(k, _):
-        give(k).wait_send()
-        return 0
-
-    lax.fori_loop(0, RING, given, 0)
     for side in range(2):
         far(side).wait_send()
         for d in range(1, 4):
             for h in range(CHAIN):
                 chain(side, d, h).wait_send()
-    if n_head > 1:
-        for got, sem in ((got_g, ga_send), (got_o, oa_send)):
-            others = got.at[pl.ds(0, n_head - 1)]
-            pltpu.make_async_copy(others, others, sem).wait()
     for store in stores:
         store.wait()
 

time: 67.6 us -> 67.7 us (level)
  no operation moved by 1% of the time
where the time goes in v4:
time: 67.7 us; the launch traced here: 67.5 us
  Pallas kernels  63.6 us (94%)
  local copies, waits for them, and re-layouts  3.18 us (5%)
    pallas_call x1, Pallas kernels, local(): pl.pallas_call(functools.partial(kernel, n_head), out_shape=(jax.ShapeDty...  63.6 us
    unnamed x7, local copies, waits for them, and re-layouts  3.18 us

profile of v4, /device:TPU:1, one launch (start us, length us, event | category | flops | bytes accessed | tf_op | source)
XLA Modules:
  0.0 67.5 jit_solution(14735621094614985147)
XLA Ops:
  0.6 63.6 %sparse_bwd.1 = (bf16[384,128]{1,0:T(8,128)(2,1)}, bf16[512,128]{1,0:T(8,128)(2,1)}, bf16[512,128]{1,0:T(8,128)(2,1)}) custom-call(bf16[384,128]{1,0:T(8,128)(2,1)} %q_hbm.1, bf16[512,128]{1,0:T(8,128)(2,1)} %k_hbm.1, bf16[512,128]{1,0:T(8,128)(2,1)} %v_hbm.1, bf16[8,6144]{1,0:T(8,128)(2,1)} %o_hbm.1, bf16[8,6144]{1,0:T(8,128)(2,1)} %g_hbm.1, ...), custom_call_target="tpu_custom_call" | custom-call | tf_op jit(solution)/shard_map/sparse_bwd/pallas_call | solution.py:441
  64.3 0.0 copy-start.1
  64.3 1.6 %copy.14 = bf16[384,128]{1,0:T(8,128)(2,1)} copy(bf16[384,128]{1,0:T(8,128)(2,1)} %get-tuple-element.6) | data formatting | bytes 196608
  65.9 0.0 copy-done.1
  65.9 0.0 copy-start
  65.9 0.7 copy.15
  66.5 0.3 copy-done
  66.8 0.7 copy.16
Async XLA Ops:
  64.3 1.6 %copy-start.1 = (bf16[512,128]{1,0:T(8,128)(2,1)S(1)}, bf16[512,128]{1,0:T(8,128)(2,1)}, u32[]{:S(2)}) copy-start(bf16[512,128]{1,0:T(8,128)(2,1)} %get-tuple-element.7) | copy-start | bytes 393220
  65.9 1.0 %copy-start = (bf16[512,128]{1,0:T(8,128)(2,1)S(1)}, bf16[512,128]{1,0:T(8,128)(2,1)}, u32[]{:S(2)}) copy-start(bf16[512,128]{1,0:T(8,128)(2,1)} %get-tuple-element.8) | copy-start | bytes 393220

commit v5 on v4

--- a/solution.py
+++ b/solution.py
@@ -155,6 +155,31 @@
             def _():
                 self.twin(RING - d).start()
 
+        def leap(self, side):
+            return pltpu.make_async_remote_copy(
+                src_ref=self.buf.at[0, 0, self.spans[side]],
+                dst_ref=self.buf.at[0, slot(side, 3), self.spans[side]],
+                send_sem=self.send.at[side, 2, side],
+                recv_sem=self.recv.at[side, 3, side],
+                device_id=far_home[1 - side],
+            )
+
+        def relay_rest(self, d):
+            for h in range(2):
+                for side in range(2):
+                    last = 2 if h == side else 3
+
+                    @pl.when(d <= last)
+                    def _():
+                        self.hop(side, d - 1, h).wait_recv()
+
+                    @pl.when(d < last)
+                    def _():
+                        self.hop(side, d, h).start()
+
+            self.twin(d).start()
+            self.twin(RING - d).start()
+
         def drain(self):
             def per_hop(d, _):
                 for h in range(2):
@@ -331,6 +356,7 @@
             pltpu.make_async_copy(got_g, got_g, ga_recv).wait()
             g = got_g[...].astype(jnp.float32).reshape(rows, dh)
             gb[0, 0, pl.ds(0, rows), :] = g.astype(jnp.bfloat16)
+            g_ring.leap(0).start()
             g_ring.start_piece(0)
             kt[...] = kx[...].astype(jnp.float32).T.astype(jnp.bfloat16)
             dk_acc[...] = jnp.zeros_like(dk_acc)
@@ -353,34 +379,47 @@
                 precision=lax.Precision.HIGHEST, preferred_element_type=jnp.float32,
             )
             gb[0, 0, pl.ds(rows, 16), :] = lane_tiles(delta[0:1, :])
+            g_ring.leap(1).start()
             g_ring.start_piece(1)
             g_ring.twin(0).start()
 
         @pl.when(t >= 3)
         def _():
-            g_ring.relay(t - 2)
+            g_ring.relay_rest(t - 2)
+
+        @pl.when(t == 5)
+        def _():
+            give(4).wait_recv()
+            for side in range(2):
+                for i in range(CHAIN // 2):
+                    far_s[side, i] = local_sum(4, side * (CHAIN // 2) + i).astype(jnp.bfloat16)
+                far(side).start()
 
         def backward(j, _):
-            backward_pair(t - 2, j)
+            @pl.when((t == 3) & (j == 1))
+            def _():
+                for side in range(2):
+                    g_ring.leap(side).wait_recv()
+                    g_ring.hop(side, 3, side).start()
+
+            @pl.when((t == 4) & (j == 1))
+            def _():
+                for side in range(2):
+                    g_ring.hop(side, 3, side).wait_recv()
+                g_ring.twin(4).start()
+
+            backward_pair(jnp.where(j == 2, 4, t - 2), j)
             return 0
 
-        @pl.when(t == 6)
-        def _():
-            send_home(3)
-
         @pl.when(t >= 2)
         def _():
-            lax.fori_loop(0, jnp.where((t == 2) | (t == 6), 1, 2), backward, 0)
+            lax.fori_loop(0, jnp.where(t == 2, 1, jnp.where(t == 4, 3, 2)), backward, 0)
 
         return 0
 
-    lax.fori_loop(0, 7, tick, 0)
-
-    give(4).wait_recv()
-    for side in range(2):
-        for i in range(CHAIN // 2):
-            far_s[side, i] = local_sum(4, side * (CHAIN // 2) + i).astype(jnp.bfloat16)
-        far(side).start()
+    lax.fori_loop(0, 6, tick, 0)
+
+    send_home(3)
 
     dk_v[...] = (dk_acc[...] * scale).astype(jnp.bfloat16)
     dv_v[...] = dv_acc[...].astype(jnp.bfloat16)

time: 67.7 us -> 67.4 us (level)
  no operation moved by 1% of the time
where the time goes in v5:
time: 67.4 us; the launch traced here: 67.2 us
  Pallas kernels  63.4 us (94%)
  local copies, waits for them, and re-layouts  3.18 us (5%)
    pallas_call x1, Pallas kernels, local(): pl.pallas_call(functools.partial(kernel, n_head), out_shape=(jax.ShapeDty...  63.4 us
    unnamed x7, local copies, waits for them, and re-layouts  3.18 us

profile of v5, /device:TPU:1, one launch (start us, length us, event | category | flops | bytes accessed | tf_op | source)
XLA Modules:
  0.0 67.2 jit_solution(1890315466182526165)
XLA Ops:
  0.6 63.4 %sparse_bwd.1 = (bf16[384,128]{1,0:T(8,128)(2,1)}, bf16[512,128]{1,0:T(8,128)(2,1)}, bf16[512,128]{1,0:T(8,128)(2,1)}) custom-call(bf16[384,128]{1,0:T(8,128)(2,1)} %q_hbm.1, bf16[512,128]{1,0:T(8,128)(2,1)} %k_hbm.1, bf16[512,128]{1,0:T(8,128)(2,1)} %v_hbm.1, bf16[8,6144]{1,0:T(8,128)(2,1)} %o_hbm.1, bf16[8,6144]{1,0:T(8,128)(2,1)} %g_hbm.1, ...), custom_call_target="tpu_custom_call" | custom-call | tf_op jit(solution)/shard_map/sparse_bwd/pallas_call | solution.py:480
  64.0 0.0 copy-start.1
  64.0 1.6 %copy.14 = bf16[384,128]{1,0:T(8,128)(2,1)} copy(bf16[384,128]{1,0:T(8,128)(2,1)} %get-tuple-element.6) | data formatting | bytes 196608
  65.6 0.0 copy-done.1
  65.6 0.0 copy-start
  65.6 0.7 copy.15
  66.3 0.3 copy-done
  66.6 0.7 copy.16
Async XLA Ops:
  64.0 1.6 %copy-start.1 = (bf16[512,128]{1,0:T(8,128)(2,1)S(1)}, bf16[512,128]{1,0:T(8,128)(2,1)}, u32[]{:S(2)}) copy-start(bf16[512,128]{1,0:T(8,128)(2,1)} %get-tuple-element.7) | copy-start | bytes 393220
  65.6 1.0 %copy-start = (bf16[512,128]{1,0:T(8,128)(2,1)S(1)}, bf16[512,128]{1,0:T(8,128)(2,1)}, u32[]{:S(2)}) copy-start(bf16[512,128]{1,0:T(8,128)(2,1)} %get-tuple-element.8) | copy-start | bytes 393220
